TPU v7x, 128 devices: a whole 4x4x4 slice. The times are simulated.
128 devices in a mesh: rows: 2 (over core), head: 4 (over x), cluster: 16 (over y, z).
Axes of the slice: x: 4, y: 4, z: 4, core: 2. Of those that a mesh axis runs over, the one named last changes fastest.
Arguments:
- queries: bfloat16 [4, 512, 8192], P(None, ('rows', 'cluster'), 'head')
- new_keys: bfloat16 [4, 512, 1024], P(None, ('rows', 'cluster'), 'head'), may hold values from -6 to 6
- new_values: bfloat16 [4, 512, 1024], P(None, ('rows', 'cluster'), 'head'), may hold values from -6 to 6
- key_cache: bfloat16 [512, 8, 256, 128], P(('rows', 'cluster'), 'head'), may hold values from -6 to 6
- value_cache: bfloat16 [512, 8, 256, 128], P(('rows', 'cluster'), 'head'), may hold values from -6 to 6
- lengths: int32 [512], P(('rows', 'cluster')), may hold values from 1 to 256, as said below
- residual_in: bfloat16 [4, 512, 8192], P(None, 'rows', 'cluster')
- out_weight: bfloat16 [8192, 8192], P('head', 'cluster'), may hold values from -0.0625 to 0.0625
- norm_gain: float32 [8192], P('cluster'), may hold values from 0.5 to 1.5
- top_weight: bfloat16 [8192, 80], P('cluster')
- leaf_weight: bfloat16 [80, 8192, 1024], P('cluster', None, ('rows', 'head'))
- cluster_ids: int32 [4, 512, 1], replicated, may hold values from 0 to 79; in each aligned block of 256 rows (0 to 255, 256 to 511, ..., all dimensions but the last counted through in order) at most 12 rows name the same one
- targets: int32 [4, 512], replicated, may hold values from 0 to 1023
Outputs:
- log_prob: float32 [4, 512], P(None, ('rows', 'cluster'))
Inputs may be any that keep to these rules, and one draw needn't show every extreme that they name: `cluster_ids`: in each step and each aligned block of 256 rows, no cluster is named by more than 12 rows, a bound that some block reaches. `lengths`: every device's 16 rows include one of length 256.
All inputs are finite; a program needn't handle non-finite values.
Results may differ from a plain program's by a relative error of at most 0.0011.
Values may be sent and summed in bfloat16 or wider, within the bound.
No kernel may reach another device: no remote copies, remote signals or barrier semaphores. Data moves between devices by JAX's collectives and lax.ppermute only.
A program may use at most 128 MiB of HBM per device.

v0:
```python
import jax
import jax.numpy as jnp
from jax import lax
from jax.sharding import PartitionSpec as P

D = 8192
CLUSTERS = 80
STEPS = 4


def merged(part, axis, combine):
    gathered = jax.tree.map(lambda a: lax.all_gather(a, axis), part)

    def take(source):
        return jax.tree.map(lambda a: lax.dynamic_index_in_dim(a, source, 0, False), gathered)

    return lax.fori_loop(
        1, lax.axis_size(axis), lambda source, state: combine(state, take(source)), take(0)
    )


def combine_totals(first, second):
    peak_a, mass_a, picked_a = first
    peak_b, mass_b, picked_b = second
    peak = jnp.maximum(peak_a, peak_b)
    mass = mass_a * jnp.exp(peak_a - peak) + mass_b * jnp.exp(peak_b - peak)
    return (peak, mass, picked_a + picked_b)


def shards(
    queries,
    new_keys,
    new_values,
    key_cache,
    value_cache,
    lengths,
    residual_in,
    out_weight,
    norm_gain,
    top_weight,
    leaf_weight,
    cluster_ids,
    targets,
):
    own_rows, kv_local, cache_len, head_dim = key_cache.shape
    group = queries.shape[2] // head_dim // kv_local
    scale = head_dim ** (-0.5)
    clusters_axis = lax.axis_size("cluster")
    row_groups = lax.axis_size("rows")
    heads_axis = lax.axis_size("head")
    row_group = own_rows * clusters_axis
    local_clusters = leaf_weight.shape[0]
    leaf_local = leaf_weight.shape[2]
    most = max(2, 4 * row_group // CLUSTERS)
    capacity = local_clusters * most
    my_cluster = lax.axis_index("cluster")
    my_row = lax.axis_index("rows")
    my_head = lax.axis_index("head")
    column_start = (my_row * heads_axis + my_head) * leaf_local
    valid = jnp.arange(cache_len)[None, :] < lengths[:, None]
    index = jnp.arange(row_group)
    slot_range = jnp.arange(capacity)
    results = []
    for step in range(STEPS):
        query = queries[step].reshape(own_rows, kv_local, group, head_dim)
        cached = (
            jnp.einsum("rkgd,rkpd->rkgp", query, key_cache, preferred_element_type=jnp.float32)
            * scale
        )
        cached = jnp.where(valid[:, None, None, :], cached, -jnp.inf)
        fresh_keys = new_keys[: step + 1].reshape(step + 1, own_rows, kv_local, head_dim)
        fresh_values = new_values[: step + 1].reshape(step + 1, own_rows, kv_local, head_dim)
        recent = (
            jnp.einsum("rkgd,srkd->rkgs", query, fresh_keys, preferred_element_type=jnp.float32)
            * scale
        )
        peak = jnp.maximum(jnp.max(cached, axis=-1), jnp.max(recent, axis=-1))
        e_cached = jnp.exp(cached - peak[..., None])
        e_recent = jnp.exp(recent - peak[..., None])
        total = jnp.sum(e_cached, axis=-1) + jnp.sum(e_recent, axis=-1)
        w_cached = (e_cached / total[..., None]).astype(jnp.bfloat16)
        w_recent = (e_recent / total[..., None]).astype(jnp.bfloat16)
        output = jnp.einsum(
            "rkgp,rkpd->rkgd", w_cached, value_cache, preferred_element_type=jnp.float32
        )
        output = output + jnp.einsum(
            "rkgs,srkd->rkgd", w_recent, fresh_values, preferred_element_type=jnp.float32
        )
        attended = output.astype(jnp.bfloat16).reshape(own_rows, kv_local * group * head_dim)
        partial_sum = jnp.dot(
            lax.all_gather(attended, "cluster", axis=0, tiled=True),
            out_weight,
            preferred_element_type=jnp.float32,
        )
        mixed = lax.psum(partial_sum, "head")
        residual_part = residual_in[step].astype(jnp.float32)
        hidden = mixed + residual_part
        squares = jnp.sum(hidden * hidden, axis=1)
        gated = (hidden * norm_gain).astype(jnp.bfloat16)
        top_partial = jnp.dot(gated, top_weight, preferred_element_type=jnp.float32)
        squares, top_logits = lax.psum((squares, top_partial), "cluster")
        inv_rms = lax.rsqrt(squares / D + 1e-05)
        top_logprob = jax.nn.log_softmax(top_logits * inv_rms[:, None], axis=-1)
        normed = (hidden * norm_gain * inv_rms[:, None]).astype(jnp.bfloat16)
        step_ids = cluster_ids[step, :, 0].reshape(row_groups, row_group)
        step_targets = targets[step].reshape(row_groups, row_group)
        earlier = (step_ids[:, :, None] == step_ids[:, None, :]) & (
            index[None, None, :] < index[None, :, None]
        )
        rank = jnp.sum(earlier.astype(jnp.int32), axis=2)
        dest = step_ids // local_clusters
        slot = step_ids % local_clusters * most + rank
        own_ids = lax.dynamic_index_in_dim(step_ids, my_row, 0, keepdims=False)
        own_dest = lax.dynamic_index_in_dim(dest, my_row, 0, keepdims=False)
        own_slot = lax.dynamic_index_in_dim(slot, my_row, 0, keepdims=False)
        top_pick = jnp.sum(
            jnp.where(jnp.arange(CLUSTERS)[None, :] == own_ids[:, None], top_logprob, 0.0), axis=1
        )
        sending = (own_dest[None, None, :] == jnp.arange(clusters_axis)[:, None, None]) & (
            own_slot[None, None, :] == slot_range[None, :, None]
        )
        outgoing = jnp.einsum(
            "dsi,if->sdf", sending.astype(jnp.bfloat16), normed, preferred_element_type=jnp.float32
        )
        outgoing = outgoing.astype(jnp.bfloat16).reshape(capacity, -1)
        arrived = lax.all_to_all(outgoing, "cluster", split_axis=1, concat_axis=1, tiled=True)
        both = lax.all_gather(arrived, "rows", axis=0, tiled=True).reshape(
            row_groups, local_clusters, most, D
        )
        logits = jnp.einsum("ncmd,cdv->ncmv", both, leaf_weight, preferred_element_type=jnp.float32)
        landing = (dest == my_cluster)[:, None, :] & (slot[:, None, :] == slot_range[None, :, None])
        slot_target = jnp.sum(jnp.where(landing, step_targets[:, None, :], 0), axis=2)
        target_here = slot_target.reshape(row_groups, local_clusters, most) - column_start
        hit = jnp.arange(leaf_local)[None, None, None, :] == target_here[..., None]
        picked = jnp.sum(jnp.where(hit, logits, 0.0), axis=-1)
        leaf_peak = jnp.max(logits, axis=-1)
        mass = jnp.sum(jnp.exp(logits - leaf_peak[..., None]), axis=-1)
        leaf_peak, mass, picked = merged(
            (leaf_peak, mass, picked), ("rows", "head"), combine_totals
        )
        leaf_logprob = (picked - leaf_peak - jnp.log(mass)).reshape(row_groups, capacity)
        own_logprob = lax.dynamic_index_in_dim(leaf_logprob, my_row, 0, keepdims=False)
        own_landing = lax.dynamic_index_in_dim(landing, my_row, 0, keepdims=False)
        spread = jnp.sum(jnp.where(own_landing, own_logprob[:, None], 0.0), axis=0)
        back = lax.psum_scatter(spread, "cluster", scatter_dimension=0, tiled=True)
        top_own = lax.dynamic_slice_in_dim(top_pick, my_cluster * own_rows, own_rows, 0)
        results.append(top_own + back)
    return jnp.stack(results, axis=0)


def solution(mesh):
    placed = (
        P(None, ("rows", "cluster"), "head"),
        P(None, ("rows", "cluster"), "head"),
        P(None, ("rows", "cluster"), "head"),
        P(("rows", "cluster"), "head", None, None),
        P(("rows", "cluster"), "head", None, None),
        P(("rows", "cluster")),
        P(None, "rows", "cluster"),
        P("head", "cluster"),
        P("cluster"),
        P("cluster", None),
        P("cluster", None, ("rows", "head")),
        P(),
        P(),
    )
    return jax.shard_map(
        shards, mesh=mesh, in_specs=placed, out_specs=P(None, ("rows", "cluster")), check_vma=False
    )
```

profile of v0, /device:TPU:2, one launch (start us, length us, event | category | flops | bytes accessed | tf_op | source)
XLA Modules:
  0.0 766.7 jit_solution(16518504707865597806)
XLA Ops:
  14.7 2.4 fusion.145
  19.1 2.4 fusion.144
  23.3 2.4 fusion.149
  28.6 30.9 %all-gather.29.cloned.1.call-done = bf16[256,2048]{1,0:T(8,128)(2,1)} async-done(((bf16[16,2048]{1,0:T(8,128)(2,1)}), bf16[256,2048]{1,0:T(8,128)(2,1)}) %all-gather.29.cloned.1.call-update) | async-done | bytes 1048592 | tf_op jit(solution)/shard_map/all_gather | solution.py:91
  59.5 2.7 fusion.158
  62.2 41.3 %all-gather.31.cloned.1.call-done = bf16[256,2048]{1,0:T(8,128)(2,1)} async-done(((bf16[16,2048]{1,0:T(8,128)(2,1)}), bf16[256,2048]{1,0:T(8,128)(2,1)}) %all-gather.31.cloned.1.call-update) | async-done | bytes 1048592 | tf_op jit(solution)/shard_map/all_gather | solution.py:91
  103.6 2.7 fusion.159
  106.3 41.3 %all-gather.25.cloned.1.call-done = bf16[256,2048]{1,0:T(8,128)(2,1)} async-done(((bf16[16,2048]{1,0:T(8,128)(2,1)}), bf16[256,2048]{1,0:T(8,128)(2,1)}) %all-gather.25.cloned.1.call-update) | async-done | bytes 1048592 | tf_op jit(solution)/shard_map/all_gather | solution.py:91
  147.6 2.7 fusion.156
  150.3 41.2 %all-gather.27.cloned.1.call-done = bf16[256,2048]{1,0:T(8,128)(2,1)} async-done(((bf16[16,2048]{1,0:T(8,128)(2,1)}), bf16[256,2048]{1,0:T(8,128)(2,1)}) %all-gather.27.cloned.1.call-update) | async-done | bytes 1048592 | tf_op jit(solution)/shard_map/all_gather | solution.py:91
  191.5 2.7 fusion.157
  195.0 56.2 %all-reduce.13.cloned.1.call-done = (f32[256,512]{1,0:T(8,128)}, f32[256,512]{1,0:T(8,128)}, f32[256,512]{1,0:T(8,128)}, f32[256,512]{1,0:T(8,128)}) async-done(((f32[256,512]{1,0:T(8,128)}, f32[256,512]{1,0:T(8,128)}, f32[256,512]{1,0:T(8,128)}, f32[256,512]{1,0:T(8,128)}), (f32[256,512]{1,0:T(8,128)}, f32[256,512]{1,0:T(8,128)}, f32[256,512]{1,0:T(8,128)}, ...) | async-done | bytes 2097168 | tf_op jit(solution)/shard_map/psum | solution.py:95
  253.0 40.6 %all-reduce.5 = (f32[256]{0:T(256)S(1)}, f32[256]{0:T(256)S(1)}, f32[256]{0:T(256)S(1)}, f32[256]{0:T(256)S(1)}) all-reduce(f32[256]{0:T(256)S(1)} %get-tuple-element.899, f32[256]{0:T(256)S(1)} %get-tuple-element.900, f32[256]{0:T(256)S(1)} %get-tuple-element.901, ...), channel_id=1, replica_groups=mesh['rows'=2,'head'=4,'cluster'=16] {'cluster'}, use_global_device_ids=true, to_apply=%region_61.63 | all-reduce | flops 1024 | bytes 8192 | tf_op jit(solution)/shard_map/psum | solution.py:101
  295.5 2.6 fusion.23
  298.1 3.7 all-to-all-start.3
  307.7 6.9 all-to-all-done.3
  316.1 2.5 reshape.625
  318.7 2.5 fusion.22
  321.1 3.7 all-to-all-start.2
  325.1 12.7 %all-to-all-done.2 = bf16[60,16,512]{2,0,1:T(8,128)(2,1)S(1)} async-done(((bf16[60,16,512]{2,0,1:T(8,128)(2,1)}), bf16[60,16,512]{2,0,1:T(8,128)(2,1)S(1)}, u32[]{:S(2)}, u32[]{:S(2)}) %all-to-all-start.2) | async-done | bytes 983072 | tf_op jit(solution)/shard_map/all_to_all | solution.py:126
  341.8 2.5 fusion.21
  344.2 3.7 all-to-all-start.1
  349.8 11.1 %all-to-all-done.1 = bf16[60,16,512]{2,0,1:T(8,128)(2,1)S(1)} async-done(((bf16[60,16,512]{2,0,1:T(8,128)(2,1)}), bf16[60,16,512]{2,0,1:T(8,128)(2,1)S(1)}, u32[]{:S(2)}, u32[]{:S(2)}) %all-to-all-start.1) | async-done | bytes 983072 | tf_op jit(solution)/shard_map/all_to_all | solution.py:126
  362.4 2.4 reshape.621
  364.9 2.5 fusion.20
  367.3 3.7 all-to-all-start
  371.0 33.0 %all-reduce.11.cloned.1.call-done = (f32[256,80]{0,1:T(8,128)}, f32[256,80]{0,1:T(8,128)}, f32[256,80]{0,1:T(8,128)}, f32[256,80]{0,1:T(8,128)}) async-done(((f32[256,80]{0,1:T(8,128)}, f32[256,80]{0,1:T(8,128)}, f32[256,80]{0,1:T(8,128)}, f32[256,80]{0,1:T(8,128)}), (f32[256,80]{0,1:T(8,128)}, f32[256,80]{0,1:T(8,128)}, f32[256,80]{0,1:T(8,128)}, f32[256,80]{0,1:T(8,128)})) %all-reduce.11.cloned.1.call-update) | async-done | bytes 327696 | tf_op jit(solution)/shard_map/psum | solution.py:101
  419.1 3.6 copy.426
  422.7 5.6 fusion.151
  428.6 21.7 %all-gather.10 = f32[16,5,12]{2,1,0:T(8,128)S(1)} all-gather(f32[2,5,12]{2,1,0:T(8,128)S(1)} %copy.429), channel_id=12, replica_groups=mesh['rows'=2,'head'=4,'cluster'=16] {'rows','head'}, dimensions={0}, use_global_device_ids=true | all-gather | bytes 4320 | tf_op jit(solution)/shard_map/all_gather | solution.py:12
  450.3 21.6 %all-gather.9 = f32[16,5,12]{2,1,0:T(8,128)S(1)} all-gather(f32[2,5,12]{2,1,0:T(8,128)S(1)} %copy.428), channel_id=11, replica_groups=mesh['rows'=2,'head'=4,'cluster'=16] {'rows','head'}, dimensions={0}, use_global_device_ids=true | all-gather | bytes 4320 | tf_op jit(solution)/shard_map/all_gather | solution.py:12
  471.9 21.7 %all-gather.11 = f32[16,5,12]{2,1,0:T(8,128)S(1)} all-gather(f32[2,5,12]{2,1,0:T(8,128)S(1)} %copy.433), channel_id=13, replica_groups=mesh['rows'=2,'head'=4,'cluster'=16] {'rows','head'}, dimensions={0}, use_global_device_ids=true | all-gather | bytes 4320 | tf_op jit(solution)/shard_map/all_gather | solution.py:12
  494.1 3.6 copy.405
  497.8 5.6 fusion.152
  503.6 21.5 %all-gather.7 = f32[16,5,12]{2,1,0:T(8,128)S(1)} all-gather(f32[2,5,12]{2,1,0:T(8,128)S(1)} %copy.408), channel_id=9, replica_groups=mesh['rows'=2,'head'=4,'cluster'=16] {'rows','head'}, dimensions={0}, use_global_device_ids=true | all-gather | bytes 4320 | tf_op jit(solution)/shard_map/all_gather | solution.py:12
  525.2 21.5 %all-gather.6 = f32[16,5,12]{2,1,0:T(8,128)S(1)} all-gather(f32[2,5,12]{2,1,0:T(8,128)S(1)} %copy.407), channel_id=8, replica_groups=mesh['rows'=2,'head'=4,'cluster'=16] {'rows','head'}, dimensions={0}, use_global_device_ids=true | all-gather | bytes 4320 | tf_op jit(solution)/shard_map/all_gather | solution.py:12
  546.7 21.5 %all-gather.8 = f32[16,5,12]{2,1,0:T(8,128)S(1)} all-gather(f32[2,5,12]{2,1,0:T(8,128)S(1)} %copy.412), channel_id=10, replica_groups=mesh['rows'=2,'head'=4,'cluster'=16] {'rows','head'}, dimensions={0}, use_global_device_ids=true | all-gather | bytes 4320 | tf_op jit(solution)/shard_map/all_gather | solution.py:12
  568.8 3.6 copy.384
  572.4 5.6 fusion.153
  578.3 21.5 %all-gather.4 = f32[16,5,12]{2,1,0:T(8,128)S(1)} all-gather(f32[2,5,12]{2,1,0:T(8,128)S(1)} %copy.387), channel_id=6, replica_groups=mesh['rows'=2,'head'=4,'cluster'=16] {'rows','head'}, dimensions={0}, use_global_device_ids=true | all-gather | bytes 4320 | tf_op jit(solution)/shard_map/all_gather | solution.py:12
  599.8 21.5 %all-gather.3 = f32[16,5,12]{2,1,0:T(8,128)S(1)} all-gather(f32[2,5,12]{2,1,0:T(8,128)S(1)} %copy.386), channel_id=5, replica_groups=mesh['rows'=2,'head'=4,'cluster'=16] {'rows','head'}, dimensions={0}, use_global_device_ids=true | all-gather | bytes 4320 | tf_op jit(solution)/shard_map/all_gather | solution.py:12
  621.4 21.8 %all-gather.5 = f32[16,5,12]{2,1,0:T(8,128)S(1)} all-gather(f32[2,5,12]{2,1,0:T(8,128)S(1)} %copy.391), channel_id=7, replica_groups=mesh['rows'=2,'head'=4,'cluster'=16] {'rows','head'}, dimensions={0}, use_global_device_ids=true | all-gather | bytes 4320 | tf_op jit(solution)/shard_map/all_gather | solution.py:12
  643.7 3.6 copy.363
  647.4 5.6 fusion.154
  653.2 21.5 %all-gather.1 = f32[16,5,12]{2,1,0:T(8,128)S(1)} all-gather(f32[2,5,12]{2,1,0:T(8,128)S(1)} %copy.366), channel_id=3, replica_groups=mesh['rows'=2,'head'=4,'cluster'=16] {'rows','head'}, dimensions={0}, use_global_device_ids=true | all-gather | bytes 4320 | tf_op jit(solution)/shard_map/all_gather | solution.py:12
  674.8 21.5 %all-gather = f32[16,5,12]{2,1,0:T(8,128)S(1)} all-gather(f32[2,5,12]{2,1,0:T(8,128)S(1)} %copy.365), channel_id=2, replica_groups=mesh['rows'=2,'head'=4,'cluster'=16] {'rows','head'}, dimensions={0}, use_global_device_ids=true | all-gather | bytes 4320 | tf_op jit(solution)/shard_map/all_gather | solution.py:12
  696.3 21.5 %all-gather.2 = f32[16,5,12]{2,1,0:T(8,128)S(1)} all-gather(f32[2,5,12]{2,1,0:T(8,128)S(1)} %copy.370), channel_id=4, replica_groups=mesh['rows'=2,'head'=4,'cluster'=16] {'rows','head'}, dimensions={0}, use_global_device_ids=true | all-gather | bytes 4320 | tf_op jit(solution)/shard_map/all_gather | solution.py:12
  718.8 40.1 %all-reduce.4 = (f32[256]{0:T(256)S(1)}, f32[256]{0:T(256)S(1)}, f32[256]{0:T(256)S(1)}, f32[256]{0:T(256)S(1)}) all-reduce(f32[256]{0:T(256)S(1)} %select_reduce_fusion.8, f32[256]{0:T(256)S(1)} %select_reduce_fusion.9, f32[256]{0:T(256)S(1)} %select_reduce_fusion.10, ...), channel_id=17, replica_groups=mesh['rows'=2,'head'=4,'cluster'=16] {'cluster'}, use_global_device_ids=true, to_apply=%region_71.73.clone | all-reduce | flops 1024 | bytes 8192
  (308 shorter events, 53.6 us)
Async XLA Ops:
  6.5 53.0 %copy-start = (bf16[2048,512]{1,0:T(8,128)(2,1)S(1)}, bf16[2048,512]{1,0:T(8,128)(2,1)}, u32[]{:S(2)}) copy-start(bf16[2048,512]{1,0:T(8,128)(2,1)} %param.29) | copy-start | bytes 6291460
  6.5 53.0 %all-gather.29.cloned.1.call-start = ((), (), s32[]{:S(2)}) async-start(), calls=%async_computation.6 | async-start | bytes 1114112 | tf_op jit(solution)/shard_map/all_gather | solution.py:91
  8.9 4.3 copy-start.12
  12.7 1.7 copy-start.7
  12.9 1.5 copy-start.8
  14.3 89.2 %all-gather.31.cloned.1.call-start = ((), (), s32[]{:S(2)}) async-start(), calls=%async_computation.7 | async-start | bytes 1114112 | tf_op jit(solution)/shard_map/all_gather | solution.py:91
  14.4 3.3 copy-start.13
  17.2 1.7 slice-start
  18.8 128.8 %all-gather.25.cloned.1.call-start = ((), (), s32[]{:S(2)}) async-start(), calls=%async_computation.4 | async-start | bytes 1114112 | tf_op jit(solution)/shard_map/all_gather | solution.py:91
  18.9 2.9 copy-start.14
  21.6 1.5 slice-start.1
  21.6 1.5 slice-start.2
  23.0 168.5 %all-gather.27.cloned.1.call-start = ((), (), s32[]{:S(2)}) async-start(), calls=%async_computation.5 | async-start | bytes 1114112 | tf_op jit(solution)/shard_map/all_gather | solution.py:91
  23.1 3.3 copy-start.15
  25.9 1.7 copy-start.10
  26.1 1.5 copy-start.11
  27.5 223.7 %all-reduce.13.cloned.1.call-start = ((), (), s32[]{:S(2)}) async-start(), calls=%async_computation.13 | async-start | bytes 4194304 | tf_op jit(solution)/shard_map/psum | solution.py:95
  150.3 100.8 %copy-start.1 = (bf16[4,256,512]{2,1,0:T(8,128)(2,1)S(1)}, bf16[4,256,512]{2,1,0:T(8,128)(2,1)}, u32[]{:S(2)}) copy-start(bf16[4,256,512]{2,1,0:T(8,128)(2,1)} %param.28) | copy-start | bytes 3145732
  194.3 99.3 %copy-start.6 = (bf16[512,80]{0,1:T(8,128)(2,1)S(1)}, bf16[512,80]{0,1:T(8,128)(2,1)}, u32[]{:S(2)}) copy-start(bf16[512,80]{0,1:T(8,128)(2,1)} %param.31) | copy-start | bytes 245764
  194.3 99.3 %copy-start.9 = (f32[512]{0:T(512)S(1)}, f32[512]{0:T(512)}, u32[]{:S(2)}) copy-start(f32[512]{0:T(512)} %param.30) | copy-start | bytes 6148
  298.1 16.5 %all-to-all-start.3 = ((bf16[60,16,512]{2,0,1:T(8,128)(2,1)}), bf16[60,16,512]{2,0,1:T(8,128)(2,1)S(1)}, u32[]{:S(2)}, u32[]{:S(2)}) async-start(bf16[60,16,512]{2,0,1:T(8,128)(2,1)} %fusion.23), calls=%async_computation.3 | async-start | bytes 2097152 | tf_op jit(solution)/shard_map/all_to_all | solution.py:126
  301.7 102.3 %all-reduce.11.cloned.1.call-start = ((), (), s32[]{:S(2)}) async-start(), calls=%async_computation.12 | async-start | bytes 655360 | tf_op jit(solution)/shard_map/psum | solution.py:101
  301.8 4.0 copy-start.3
  307.6 111.5 %all-gather.39.cloned.1.call-start = ((), (), s32[]{:S(2)}) async-start(), calls=%async_computation.11 | async-start | bytes 3145728 | tf_op jit(solution)/shard_map/all_gather | solution.py:127
  316.1 2.6 copy-start.5
  321.1 16.6 %all-to-all-start.2 = ((bf16[60,16,512]{2,0,1:T(8,128)(2,1)}), bf16[60,16,512]{2,0,1:T(8,128)(2,1)S(1)}, u32[]{:S(2)}, u32[]{:S(2)}) async-start(bf16[60,16,512]{2,0,1:T(8,128)(2,1)} %fusion.22), calls=%async_computation.2 | async-start | bytes 2097152 | tf_op jit(solution)/shard_map/all_to_all | solution.py:126
  324.8 169.3 %all-gather.37.cloned.1.call-start = ((), (), s32[]{:S(2)}) async-start(), calls=%async_computation.10 | async-start | bytes 3145728 | tf_op jit(solution)/shard_map/all_gather | solution.py:127
  339.3 2.5 copy-start.4
  341.8 6.5 copy-start.16
  344.2 16.7 %all-to-all-start.1 = ((bf16[60,16,512]{2,0,1:T(8,128)(2,1)}), bf16[60,16,512]{2,0,1:T(8,128)(2,1)S(1)}, u32[]{:S(2)}, u32[]{:S(2)}) async-start(bf16[60,16,512]{2,0,1:T(8,128)(2,1)} %fusion.21), calls=%async_computation.1 | async-start | bytes 2097152 | tf_op jit(solution)/shard_map/all_to_all | solution.py:126
  347.9 220.9 %all-gather.35.cloned.1.call-start = ((), (), s32[]{:S(2)}) async-start(), calls=%async_computation.9 | async-start | bytes 3145728 | tf_op jit(solution)/shard_map/all_gather | solution.py:127
  362.4 2.5 copy-start.2
  367.3 47.8 %all-to-all-start = ((bf16[60,16,512]{2,0,1:T(8,128)(2,1)}), bf16[60,16,512]{2,0,1:T(8,128)(2,1)S(1)}, u32[]{:S(2)}, u32[]{:S(2)}) async-start(bf16[60,16,512]{2,0,1:T(8,128)(2,1)} %fusion.20), calls=%async_computation | async-start | bytes 2097152 | tf_op jit(solution)/shard_map/all_to_all | solution.py:126
  371.0 272.7 %all-gather.33.cloned.1.call-start = ((), (), s32[]{:S(2)}) async-start(), calls=%async_computation.8 | async-start | bytes 3145728 | tf_op jit(solution)/shard_map/all_gather | solution.py:127
Sparse Core Ops, SparseCore 0:
  14.5 45.0 all-gather.28
  61.6 41.8 all-gather.30
  105.7 41.8 all-gather.24
  149.6 41.8 all-gather.26
  194.4 56.7 all-reduce.12
  307.7 96.2 all-reduce.10
  405.7 12.7 all-gather.38
  420.1 14.6 all-gather.36
  436.4 14.6 all-gather.34
  452.5 14.6 all-gather.32
where the time goes:
time: 769 us; the launch traced here: 767 us
  blocking collectives  340 us (44%)
  waiting for transfers between devices  275 us (36%)
  matrix products  63.8 us (8%)
  local copies, waits for them, and re-layouts  37.6 us (5%)
  other arithmetic  19.9 us (3%)
  between operations  15.3 us (2%)
  starting transfers between devices  15.2 us (2%)
    all_gather x12, blocking collectives, merged(): gathered = jax.tree.map(lambda a: lax.all_gather(a, axis), part)  259 us
    all_gather x4, waiting for transfers between devices, shards(): lax.all_gather(attended, 'cluster', axis=0, tiled=True)  155 us
    psum x1, waiting for transfers between devices, shards(): mixed = lax.psum(partial_sum, 'head')  56.2 us
    psum x1, blocking collectives, shards(): squares, top_logits = lax.psum((squares, top_partial), 'cluster')  40.6 us
    unnamed x1, blocking collectives  40.1 us
    psum x1, waiting for transfers between devices, shards(): squares, top_logits = lax.psum((squares, top_partial), 'cluster')  33 us
    all_to_all x4, waiting for transfers between devices, shards(): lax.all_to_all(outgoing, 'cluster', split_axis=1, concat_axis=1, tiled=True)  30.7 us
    dot_general x4, matrix products, shards(): jnp.einsum('ncmd,cdv->ncmv', both, leaf_weight, preferred_element_type=jn...  22.4 us
  transfers between devices with their start and end apart: 14, of which 9 were waited for; matrix products, arithmetic and copies ran while one was open for 12% of the time, Pallas kernels for 0%

commit v1 on v0

--- a/solution.py
+++ b/solution.py
@@ -1,3 +1,4 @@
+import functools
 import jax
 import jax.numpy as jnp
 from jax import lax
@@ -6,6 +7,31 @@
 D = 8192
 CLUSTERS = 80
 STEPS = 4
+
+
+def refer_the_tiles(chunk, d0):
+    t_next = lax.axis_size("cluster")
+    y_new, vec_out, all_values = (t_next, lax.axis_index("cluster"), chunk.shape[d0])
+    so_far_all = tuple(((w, (w + 1) % y_new) for w in range(y_new)))
+    kept_rows = tuple(((w, (w - 1) % y_new) for w in range(y_new)))
+    y = jnp.zeros((*chunk.shape[:d0], y_new * all_values, *chunk.shape[d0 + 1 :]), chunk.dtype)
+    y = lax.dynamic_update_slice_in_dim(y, chunk, vec_out * all_values, axis=d0)
+    latest = block_out = chunk
+    local_out = y_new // 2
+    at = 1
+    while at < local_out + 1:
+        latest = lax.ppermute(latest, axis_name="cluster", perm=so_far_all)
+        y = lax.dynamic_update_slice_in_dim(y, latest, (vec_out - at) % y_new * all_values, axis=d0)
+        if at < y_new - local_out:
+            block_out = lax.ppermute(block_out, perm=kept_rows, axis_name="cluster")
+            y = lax.dynamic_update_slice_in_dim(
+                y, block_out, (vec_out + at) % y_new * all_values, axis=d0
+            )
+        at = at + 1
+    return y
+
+
+case_search = functools.partial(refer_the_tiles, d0=0)
 
 
 def merged(part, axis, combine):
@@ -87,11 +113,7 @@
             "rkgs,srkd->rkgd", w_recent, fresh_values, preferred_element_type=jnp.float32
         )
         attended = output.astype(jnp.bfloat16).reshape(own_rows, kv_local * group * head_dim)
-        partial_sum = jnp.dot(
-            lax.all_gather(attended, "cluster", axis=0, tiled=True),
-            out_weight,
-            preferred_element_type=jnp.float32,
-        )
+        partial_sum = jnp.dot(case_search(attended), out_weight, preferred_element_type=jnp.float32)
         mixed = lax.psum(partial_sum, "head")
         residual_part = residual_in[step].astype(jnp.float32)
         hidden = mixed + residual_part

time: 769 us -> 809 us (1.052)
  starting transfers between devices: 15.2 us -> 167 us
  waiting for transfers between devices: 275 us -> 131 us
  local copies, waits for them, and re-layouts: 37.6 us -> 64.4 us
    all_gather x4 -> x0, waiting for transfers between devices: 155 us -> none  [shards(): lax.all_gather(attended, 'cluster', axis=0, tiled=True)]
    ppermute x0 -> x60, starting transfers between devices: none -> 152 us  [the longest x28 149 us: refer_the_tiles(): block_out = lax.ppermute(block_out, perm=kept_rows, axis_name='cluster')]
    dynamic_update_slice x0 -> x64, local copies, waits for them, and re-layouts: none -> 31.9 us  [the longest x32 16.3 us: refer_the_tiles(): lax.dynamic_update_slice_in_dim(y, latest, (vec_out - at) % y_new * all_v...]
  transfers between devices with their start and end apart: 14 -> 70, of which waited for: 9 -> 8; matrix products, arithmetic and copies ran while one was open for 12% -> 14% of each run, Pallas kernels for 0% -> 0%
where the time goes in v1:
time: 809 us; the launch traced here: 799 us
  blocking collectives  340 us (42%)
  starting transfers between devices  167 us (21%)
  waiting for transfers between devices  131 us (16%)
  local copies, waits for them, and re-layouts  64.4 us (8%)
  matrix products  57.9 us (7%)
  other arithmetic  21 us (3%)
  between operations  15.9 us (2%)
    all_gather x12, blocking collectives, merged(): gathered = jax.tree.map(lambda a: lax.all_gather(a, axis), part)  259 us
    ppermute x28, starting transfers between devices, refer_the_tiles(): block_out = lax.ppermute(block_out, perm=kept_rows, axis_name='cluster')  149 us
    psum x1, waiting for transfers between devices, shards(): mixed = lax.psum(partial_sum, 'head')  55.5 us
    psum x1, blocking collectives, shards(): squares, top_logits = lax.psum((squares, top_partial), 'cluster')  40.6 us
    unnamed x1, blocking collectives  40.6 us
    psum x1, waiting for transfers between devices, shards(): squares, top_logits = lax.psum((squares, top_partial), 'cluster')  37 us
    all_to_all x4, waiting for transfers between devices, shards(): lax.all_to_all(outgoing, 'cluster', split_axis=1, concat_axis=1, tiled=True)  32.9 us
    dot_general x4, matrix products, shards(): jnp.einsum('ncmd,cdv->ncmv', both, leaf_weight, preferred_element_type=jn...  22.3 us
  transfers between devices with their start and end apart: 70, of which 8 were waited for; matrix products, arithmetic and copies ran while one was open for 14% of the time, Pallas kernels for 0%

profile of v1, /device:TPU:2, one launch (start us, length us, event | category | flops | bytes accessed | tf_op | source)
XLA Modules:
  0.0 798.7 jit_solution(9253531012051287498)
XLA Ops:
  26.5 5.3 collective-permute-start.31
  46.1 5.4 collective-permute-start.46
  53.9 5.3 collective-permute-start.1
  61.6 5.3 collective-permute-start.18
  69.1 5.3 collective-permute-start.33
  75.7 5.3 collective-permute-start.48
  81.9 5.3 collective-permute-start.3
  88.0 5.3 collective-permute-start.20
  94.6 5.3 collective-permute-start.35
  101.2 5.3 collective-permute-start.50
  107.3 5.3 collective-permute-start.5
  113.3 5.3 collective-permute-start.22
  119.9 5.3 collective-permute-start.37
  126.5 5.3 collective-permute-start.52
  132.6 5.3 collective-permute-start.7
  138.6 5.3 collective-permute-start.24
  145.2 5.3 collective-permute-start.39
  151.8 5.3 collective-permute-start.54
  170.5 5.3 collective-permute-start.41
  177.1 5.5 collective-permute-start.56
  183.4 5.3 collective-permute-start.11
  189.5 5.3 collective-permute-start.28
  196.1 5.4 collective-permute-start.43
  202.7 5.3 collective-permute-start.58
  208.7 5.3 collective-permute-start.13
  230.5 55.5 %all-reduce.13.cloned.1.call-done = (f32[256,512]{1,0:T(8,128)}, f32[256,512]{1,0:T(8,128)}, f32[256,512]{1,0:T(8,128)}, f32[256,512]{1,0:T(8,128)}) async-done(((f32[256,512]{1,0:T(8,128)}, f32[256,512]{1,0:T(8,128)}, f32[256,512]{1,0:T(8,128)}, f32[256,512]{1,0:T(8,128)}), (f32[256,512]{1,0:T(8,128)}, f32[256,512]{1,0:T(8,128)}, f32[256,512]{1,0:T(8,128)}, ...) | async-done | bytes 2097168 | tf_op jit(solution)/shard_map/psum | solution.py:117
  287.9 40.6 %all-reduce.5 = (f32[256]{0:T(256)S(1)}, f32[256]{0:T(256)S(1)}, f32[256]{0:T(256)S(1)}, f32[256]{0:T(256)S(1)}) all-reduce(f32[256]{0:T(256)S(1)} %get-tuple-element.899, f32[256]{0:T(256)S(1)} %get-tuple-element.900, f32[256]{0:T(256)S(1)} %get-tuple-element.901, ...), channel_id=1, replica_groups=mesh['rows'=2,'head'=4,'cluster'=16] {'cluster'}, use_global_device_ids=true, to_apply=%region_61.63 | all-reduce | flops 1024 | bytes 8192 | tf_op jit(solution)/shard_map/psum | solution.py:123
  338.5 9.1 %all-to-all-done = bf16[60,16,512]{2,0,1:T(8,128)(2,1)S(1)} async-done(((bf16[60,16,512]{2,0,1:T(8,128)(2,1)}), bf16[60,16,512]{2,0,1:T(8,128)(2,1)S(1)}, u32[]{:S(2)}, u32[]{:S(2)}) %all-to-all-start) | async-done | bytes 983072 | tf_op jit(solution)/shard_map/all_to_all | solution.py:148
  356.5 12.4 %all-to-all-done.1 = bf16[60,16,512]{2,0,1:T(8,128)(2,1)S(1)} async-done(((bf16[60,16,512]{2,0,1:T(8,128)(2,1)}), bf16[60,16,512]{2,0,1:T(8,128)(2,1)S(1)}, u32[]{:S(2)}, u32[]{:S(2)}) %all-to-all-start.1) | async-done | bytes 983072 | tf_op jit(solution)/shard_map/all_to_all | solution.py:148
  379.1 11.4 %all-to-all-done.2 = bf16[60,16,512]{2,0,1:T(8,128)(2,1)S(1)} async-done(((bf16[60,16,512]{2,0,1:T(8,128)(2,1)}), bf16[60,16,512]{2,0,1:T(8,128)(2,1)S(1)}, u32[]{:S(2)}, u32[]{:S(2)}) %all-to-all-start.2) | async-done | bytes 983072 | tf_op jit(solution)/shard_map/all_to_all | solution.py:148
  398.9 37.0 %all-reduce.11.cloned.1.call-done = (f32[256,80]{0,1:T(8,128)}, f32[256,80]{0,1:T(8,128)}, f32[256,80]{0,1:T(8,128)}, f32[256,80]{0,1:T(8,128)}) async-done(((f32[256,80]{0,1:T(8,128)}, f32[256,80]{0,1:T(8,128)}, f32[256,80]{0,1:T(8,128)}, f32[256,80]{0,1:T(8,128)}), (f32[256,80]{0,1:T(8,128)}, f32[256,80]{0,1:T(8,128)}, f32[256,80]{0,1:T(8,128)}, f32[256,80]{0,1:T(8,128)})) %all-reduce.11.cloned.1.call-update) | async-done | bytes 327696 | tf_op jit(solution)/shard_map/psum | solution.py:123
  454.0 5.5 fusion.154
  459.7 21.9 %all-gather.1 = f32[16,5,12]{2,1,0:T(8,128)S(1)} all-gather(f32[2,5,12]{2,1,0:T(8,128)S(1)} %copy.366), channel_id=3, replica_groups=mesh['rows'=2,'head'=4,'cluster'=16] {'rows','head'}, dimensions={0}, use_global_device_ids=true | all-gather | bytes 4320 | tf_op jit(solution)/shard_map/all_gather | solution.py:38
  481.7 21.5 %all-gather.2 = f32[16,5,12]{2,1,0:T(8,128)S(1)} all-gather(f32[2,5,12]{2,1,0:T(8,128)S(1)} %copy.370), channel_id=4, replica_groups=mesh['rows'=2,'head'=4,'cluster'=16] {'rows','head'}, dimensions={0}, use_global_device_ids=true | all-gather | bytes 4320 | tf_op jit(solution)/shard_map/all_gather | solution.py:38
  503.3 21.7 %all-gather = f32[16,5,12]{2,1,0:T(8,128)S(1)} all-gather(f32[2,5,12]{2,1,0:T(8,128)S(1)} %copy.365), channel_id=2, replica_groups=mesh['rows'=2,'head'=4,'cluster'=16] {'rows','head'}, dimensions={0}, use_global_device_ids=true | all-gather | bytes 4320 | tf_op jit(solution)/shard_map/all_gather | solution.py:38
  529.1 5.5 fusion.153
  534.9 21.5 %all-gather.4 = f32[16,5,12]{2,1,0:T(8,128)S(1)} all-gather(f32[2,5,12]{2,1,0:T(8,128)S(1)} %copy.387), channel_id=6, replica_groups=mesh['rows'=2,'head'=4,'cluster'=16] {'rows','head'}, dimensions={0}, use_global_device_ids=true | all-gather | bytes 4320 | tf_op jit(solution)/shard_map/all_gather | solution.py:38
  556.5 21.5 %all-gather.5 = f32[16,5,12]{2,1,0:T(8,128)S(1)} all-gather(f32[2,5,12]{2,1,0:T(8,128)S(1)} %copy.391), channel_id=7, replica_groups=mesh['rows'=2,'head'=4,'cluster'=16] {'rows','head'}, dimensions={0}, use_global_device_ids=true | all-gather | bytes 4320 | tf_op jit(solution)/shard_map/all_gather | solution.py:38
  578.0 21.5 %all-gather.3 = f32[16,5,12]{2,1,0:T(8,128)S(1)} all-gather(f32[2,5,12]{2,1,0:T(8,128)S(1)} %copy.386), channel_id=5, replica_groups=mesh['rows'=2,'head'=4,'cluster'=16] {'rows','head'}, dimensions={0}, use_global_device_ids=true | all-gather | bytes 4320 | tf_op jit(solution)/shard_map/all_gather | solution.py:38
  603.7 5.5 fusion.152
  609.5 21.5 %all-gather.7 = f32[16,5,12]{2,1,0:T(8,128)S(1)} all-gather(f32[2,5,12]{2,1,0:T(8,128)S(1)} %copy.408), channel_id=9, replica_groups=mesh['rows'=2,'head'=4,'cluster'=16] {'rows','head'}, dimensions={0}, use_global_device_ids=true | all-gather | bytes 4320 | tf_op jit(solution)/shard_map/all_gather | solution.py:38
  631.0 21.5 %all-gather.8 = f32[16,5,12]{2,1,0:T(8,128)S(1)} all-gather(f32[2,5,12]{2,1,0:T(8,128)S(1)} %copy.412), channel_id=10, replica_groups=mesh['rows'=2,'head'=4,'cluster'=16] {'rows','head'}, dimensions={0}, use_global_device_ids=true | all-gather | bytes 4320 | tf_op jit(solution)/shard_map/all_gather | solution.py:38
  652.6 21.7 %all-gather.6 = f32[16,5,12]{2,1,0:T(8,128)S(1)} all-gather(f32[2,5,12]{2,1,0:T(8,128)S(1)} %copy.407), channel_id=8, replica_groups=mesh['rows'=2,'head'=4,'cluster'=16] {'rows','head'}, dimensions={0}, use_global_device_ids=true | all-gather | bytes 4320 | tf_op jit(solution)/shard_map/all_gather | solution.py:38
  678.5 5.7 fusion.151
  684.5 21.5 %all-gather.10 = f32[16,5,12]{2,1,0:T(8,128)S(1)} all-gather(f32[2,5,12]{2,1,0:T(8,128)S(1)} %copy.429), channel_id=12, replica_groups=mesh['rows'=2,'head'=4,'cluster'=16] {'rows','head'}, dimensions={0}, use_global_device_ids=true | all-gather | bytes 4320 | tf_op jit(solution)/shard_map/all_gather | solution.py:38
  706.1 21.5 %all-gather.11 = f32[16,5,12]{2,1,0:T(8,128)S(1)} all-gather(f32[2,5,12]{2,1,0:T(8,128)S(1)} %copy.433), channel_id=13, replica_groups=mesh['rows'=2,'head'=4,'cluster'=16] {'rows','head'}, dimensions={0}, use_global_device_ids=true | all-gather | bytes 4320 | tf_op jit(solution)/shard_map/all_gather | solution.py:38
  727.6 21.5 %all-gather.9 = f32[16,5,12]{2,1,0:T(8,128)S(1)} all-gather(f32[2,5,12]{2,1,0:T(8,128)S(1)} %copy.428), channel_id=11, replica_groups=mesh['rows'=2,'head'=4,'cluster'=16] {'rows','head'}, dimensions={0}, use_global_device_ids=true | all-gather | bytes 4320 | tf_op jit(solution)/shard_map/all_gather | solution.py:38
  750.1 40.6 %all-reduce.4 = (f32[256]{0:T(256)S(1)}, f32[256]{0:T(256)S(1)}, f32[256]{0:T(256)S(1)}, f32[256]{0:T(256)S(1)}) all-reduce(f32[256]{0:T(256)S(1)} %select_reduce_fusion.8, f32[256]{0:T(256)S(1)} %select_reduce_fusion.9, f32[256]{0:T(256)S(1)} %select_reduce_fusion.10, ...), channel_id=17, replica_groups=mesh['rows'=2,'head'=4,'cluster'=16] {'cluster'}, use_global_device_ids=true, to_apply=%region_71.73.clone | all-reduce | flops 1024 | bytes 8192
  (497 shorter events, 162.2 us)
Async XLA Ops:
  6.5 279.5 %all-reduce.13.cloned.1.call-start = ((), (), s32[]{:S(2)}) async-start(), calls=%async_computation.9 | async-start | bytes 4194304 | tf_op jit(solution)/shard_map/psum | solution.py:117
  15.7 30.4 %collective-permute-start.15 = (bf16[16,2048]{1,0:T(8,128)(2,1)}, bf16[16,2048]{1,0:T(8,128)(2,1)}, u32[]{:S(2)}, u32[]{:S(2)}) collective-permute-start(bf16[16,2048]{1,0:T(8,128)(2,1)} %bitcast.285), channel_id=1, source_target_pairs={{0,1},{1,2},{2,3},{3,4},{4,5},{5,6},{6,7},{7,8},{8,9},{9,10},{10,1... | collective-permute-start | bytes 196616 | tf_op jit(solution)/shard_map/ppermute | solution.py:23
  17.6 36.3 %collective-permute-start.16 = (bf16[16,2048]{1,0:T(8,128)(2,1)}, bf16[16,2048]{1,0:T(8,128)(2,1)}, u32[]{:S(2)}, u32[]{:S(2)}) collective-permute-start(bf16[16,2048]{1,0:T(8,128)(2,1)} %bitcast.285), channel_id=1, source_target_pairs={{0,15},{1,0},{2,1},{3,2},{4,3},{5,4},{6,5},{7,6},{8,7},{9,8},{10,9... | collective-permute-start | bytes 196616 | tf_op jit(solution)/shard_map/ppermute | solution.py:26
  26.5 25.9 %collective-permute-start.30 = (bf16[16,2048]{1,0:T(8,128)(2,1)}, bf16[16,2048]{1,0:T(8,128)(2,1)}, u32[]{:S(2)}, u32[]{:S(2)}) collective-permute-start(bf16[16,2048]{1,0:T(8,128)(2,1)} %bitcast.284), channel_id=1, source_target_pairs={{0,1},{1,2},{2,3},{3,4},{4,5},{5,6},{6,7},{7,8},{8,9},{9,10},{10,1... | collective-permute-start | bytes 196616 | tf_op jit(solution)/shard_map/ppermute | solution.py:23
  26.5 33.6 %collective-permute-start.31 = (bf16[16,2048]{1,0:T(8,128)(2,1)}, bf16[16,2048]{1,0:T(8,128)(2,1)}, u32[]{:S(2)}, u32[]{:S(2)}) collective-permute-start(bf16[16,2048]{1,0:T(8,128)(2,1)} %bitcast.284), channel_id=1, source_target_pairs={{0,15},{1,0},{2,1},{3,2},{4,3},{5,4},{6,5},{7,6},{8,7},{9,8},{10,9... | collective-permute-start | bytes 196616 | tf_op jit(solution)/shard_map/ppermute | solution.py:26
  36.3 25.4 %collective-permute-start.45 = (bf16[16,2048]{1,0:T(8,128)(2,1)}, bf16[16,2048]{1,0:T(8,128)(2,1)}, u32[]{:S(2)}, u32[]{:S(2)}) collective-permute-start(bf16[16,2048]{1,0:T(8,128)(2,1)} %bitcast.283), channel_id=1, source_target_pairs={{0,1},{1,2},{2,3},{3,4},{4,5},{5,6},{6,7},{7,8},{8,9},{9,10},{10,1... | collective-permute-start | bytes 196616 | tf_op jit(solution)/shard_map/ppermute | solution.py:23
  46.1 22.3 %collective-permute-start.46 = (bf16[16,2048]{1,0:T(8,128)(2,1)}, bf16[16,2048]{1,0:T(8,128)(2,1)S(1)}, u32[]{:S(2)}, u32[]{:S(2)}) collective-permute-start(bf16[16,2048]{1,0:T(8,128)(2,1)} %bitcast.283), channel_id=1, source_target_pairs={{0,15},{1,0},{2,1},{3,2},{4,3},{5,4},{6,5},{7,6},{8,7},{9,8},{10,9... | collective-permute-start | bytes 196616 | tf_op jit(solution)/shard_map/ppermute | solution.py:26
  52.4 16.7 %collective-permute-start = (bf16[16,2048]{1,0:T(8,128)(2,1)S(1)}, bf16[16,2048]{1,0:T(8,128)(2,1)S(1)}, u32[]{:S(2)}, u32[]{:S(2)}) collective-permute-start(bf16[16,2048]{1,0:T(8,128)(2,1)S(1)} %bitcast.329), channel_id=1, source_target_pairs={{0,1},{1,2},{2,3},{3,4},{4,5},{5,6},{6,7},{7,8},{8,9},{9,10},{10,1... | collective-permute-start | bytes 196616 | tf_op jit(solution)/shard_map/ppermute | solution.py:23
  53.9 21.1 %collective-permute-start.1 = (bf16[16,2048]{1,0:T(8,128)(2,1)S(1)}, bf16[16,2048]{1,0:T(8,128)(2,1)S(1)}, u32[]{:S(2)}, u32[]{:S(2)}) collective-permute-start(bf16[16,2048]{1,0:T(8,128)(2,1)S(1)} %bitcast.330), channel_id=1, source_target_pairs={{0,15},{1,0},{2,1},{3,2},{4,3},{5,4},{6,5},{7,6},{8,7},{9,8},{10,9... | collective-permute-start | bytes 196616 | tf_op jit(solution)/shard_map/ppermute | solution.py:26
  60.1 15.6 %collective-permute-start.17 = (bf16[16,2048]{1,0:T(8,128)(2,1)}, bf16[16,2048]{1,0:T(8,128)(2,1)S(1)}, u32[]{:S(2)}, u32[]{:S(2)}) collective-permute-start(bf16[16,2048]{1,0:T(8,128)(2,1)} %collective-permute-done.15), channel_id=1, source_target_pairs={{0,1},{1,2},{2,3},{3,4},{4,5},{5,6},{6,7},{7,8},{8,9},{9,10},{10,1... | collective-permute-start | bytes 196616 | tf_op jit(solution)/shard_map/ppermute | solution.py:23
  61.6 20.3 %collective-permute-start.18 = (bf16[16,2048]{1,0:T(8,128)(2,1)}, bf16[16,2048]{1,0:T(8,128)(2,1)S(1)}, u32[]{:S(2)}, u32[]{:S(2)}) collective-permute-start(bf16[16,2048]{1,0:T(8,128)(2,1)} %collective-permute-done.16), channel_id=1, source_target_pairs={{0,15},{1,0},{2,1},{3,2},{4,3},{5,4},{6,5},{7,6},{8,7},{9,8},{10,9... | collective-permute-start | bytes 196616 | tf_op jit(solution)/shard_map/ppermute | solution.py:26
  69.1 18.2 %collective-permute-start.33 = (bf16[16,2048]{1,0:T(8,128)(2,1)}, bf16[16,2048]{1,0:T(8,128)(2,1)S(1)}, u32[]{:S(2)}, u32[]{:S(2)}) collective-permute-start(bf16[16,2048]{1,0:T(8,128)(2,1)} %collective-permute-done.31), channel_id=1, source_target_pairs={{0,15},{1,0},{2,1},{3,2},{4,3},{5,4},{6,5},{7,6},{8,7},{9,8},{10,9... | collective-permute-start | bytes 196616 | tf_op jit(solution)/shard_map/ppermute | solution.py:26
  75.7 18.3 %collective-permute-start.48 = (bf16[16,2048]{1,0:T(8,128)(2,1)S(1)}, bf16[16,2048]{1,0:T(8,128)(2,1)S(1)}, u32[]{:S(2)}, u32[]{:S(2)}) collective-permute-start(bf16[16,2048]{1,0:T(8,128)(2,1)S(1)} %collective-permute-done.46), channel_id=1, source_target_pairs={{0,15},{1,0},{2,1},{3,2},{4,3},{5,4},{6,5},{7,6},{8,7},{9,8},{10,9... | collective-permute-start | bytes 196616 | tf_op jit(solution)/shard_map/ppermute | solution.py:26
  81.0 13.5 %collective-permute-start.2 = (bf16[16,2048]{1,0:T(8,128)(2,1)S(1)}, bf16[16,2048]{1,0:T(8,128)(2,1)S(1)}, u32[]{:S(2)}, u32[]{:S(2)}) collective-permute-start(bf16[16,2048]{1,0:T(8,128)(2,1)S(1)} %collective-permute-done), channel_id=1, source_target_pairs={{0,1},{1,2},{2,3},{3,4},{4,5},{5,6},{6,7},{7,8},{8,9},{9,10},{10,1... | collective-permute-start | bytes 196616 | tf_op jit(solution)/shard_map/ppermute | solution.py:23
  81.9 18.6 %collective-permute-start.3 = (bf16[16,2048]{1,0:T(8,128)(2,1)S(1)}, bf16[16,2048]{1,0:T(8,128)(2,1)S(1)}, u32[]{:S(2)}, u32[]{:S(2)}) collective-permute-start(bf16[16,2048]{1,0:T(8,128)(2,1)S(1)} %collective-permute-done.1), channel_id=1, source_target_pairs={{0,15},{1,0},{2,1},{3,2},{4,3},{5,4},{6,5},{7,6},{8,7},{9,8},{10,9... | collective-permute-start | bytes 196616 | tf_op jit(solution)/shard_map/ppermute | solution.py:26
  87.3 13.9 %collective-permute-start.19 = (bf16[16,2048]{1,0:T(8,128)(2,1)S(1)}, bf16[16,2048]{1,0:T(8,128)(2,1)S(1)}, u32[]{:S(2)}, u32[]{:S(2)}) collective-permute-start(bf16[16,2048]{1,0:T(8,128)(2,1)S(1)} %collective-permute-done.17), channel_id=1, source_target_pairs={{0,1},{1,2},{2,3},{3,4},{4,5},{5,6},{6,7},{7,8},{8,9},{9,10},{10,1... | collective-permute-start | bytes 196616 | tf_op jit(solution)/shard_map/ppermute | solution.py:23
  88.0 19.3 %collective-permute-start.20 = (bf16[16,2048]{1,0:T(8,128)(2,1)S(1)}, bf16[16,2048]{1,0:T(8,128)(2,1)S(1)}, u32[]{:S(2)}, u32[]{:S(2)}) collective-permute-start(bf16[16,2048]{1,0:T(8,128)(2,1)S(1)} %collective-permute-done.18), channel_id=1, source_target_pairs={{0,15},{1,0},{2,1},{3,2},{4,3},{5,4},{6,5},{7,6},{8,7},{9,8},{10,9... | collective-permute-start | bytes 196616 | tf_op jit(solution)/shard_map/ppermute | solution.py:26
  94.6 18.0 %collective-permute-start.35 = (bf16[16,2048]{1,0:T(8,128)(2,1)S(1)}, bf16[16,2048]{1,0:T(8,128)(2,1)S(1)}, u32[]{:S(2)}, u32[]{:S(2)}) collective-permute-start(bf16[16,2048]{1,0:T(8,128)(2,1)S(1)} %collective-permute-done.33), channel_id=1, source_target_pairs={{0,15},{1,0},{2,1},{3,2},{4,3},{5,4},{6,5},{7,6},{8,7},{9,8},{10,9... | collective-permute-start | bytes 196616 | tf_op jit(solution)/shard_map/ppermute | solution.py:26
  101.2 18.1 %collective-permute-start.50 = (bf16[16,2048]{1,0:T(8,128)(2,1)S(1)}, bf16[16,2048]{1,0:T(8,128)(2,1)S(1)}, u32[]{:S(2)}, u32[]{:S(2)}) collective-permute-start(bf16[16,2048]{1,0:T(8,128)(2,1)S(1)} %collective-permute-done.48), channel_id=1, source_target_pairs={{0,15},{1,0},{2,1},{3,2},{4,3},{5,4},{6,5},{7,6},{8,7},{9,8},{10,9... | collective-permute-start | bytes 196616 | tf_op jit(solution)/shard_map/ppermute | solution.py:26
  107.3 18.6 %collective-permute-start.5 = (bf16[16,2048]{1,0:T(8,128)(2,1)S(1)}, bf16[16,2048]{1,0:T(8,128)(2,1)S(1)}, u32[]{:S(2)}, u32[]{:S(2)}) collective-permute-start(bf16[16,2048]{1,0:T(8,128)(2,1)S(1)} %collective-permute-done.3), channel_id=1, source_target_pairs={{0,15},{1,0},{2,1},{3,2},{4,3},{5,4},{6,5},{7,6},{8,7},{9,8},{10,9... | collective-permute-start | bytes 196616 | tf_op jit(solution)/shard_map/ppermute | solution.py:26
  112.6 13.9 %collective-permute-start.21 = (bf16[16,2048]{1,0:T(8,128)(2,1)S(1)}, bf16[16,2048]{1,0:T(8,128)(2,1)S(1)}, u32[]{:S(2)}, u32[]{:S(2)}) collective-permute-start(bf16[16,2048]{1,0:T(8,128)(2,1)S(1)} %collective-permute-done.19), channel_id=1, source_target_pairs={{0,1},{1,2},{2,3},{3,4},{4,5},{5,6},{6,7},{7,8},{8,9},{9,10},{10,1... | collective-permute-start | bytes 196616 | tf_op jit(solution)/shard_map/ppermute | solution.py:23
  113.3 19.3 %collective-permute-start.22 = (bf16[16,2048]{1,0:T(8,128)(2,1)S(1)}, bf16[16,2048]{1,0:T(8,128)(2,1)S(1)}, u32[]{:S(2)}, u32[]{:S(2)}) collective-permute-start(bf16[16,2048]{1,0:T(8,128)(2,1)S(1)} %collective-permute-done.20), channel_id=1, source_target_pairs={{0,15},{1,0},{2,1},{3,2},{4,3},{5,4},{6,5},{7,6},{8,7},{9,8},{10,9... | collective-permute-start | bytes 196616 | tf_op jit(solution)/shard_map/ppermute | solution.py:26
  119.9 18.0 %collective-permute-start.37 = (bf16[16,2048]{1,0:T(8,128)(2,1)S(1)}, bf16[16,2048]{1,0:T(8,128)(2,1)S(1)}, u32[]{:S(2)}, u32[]{:S(2)}) collective-permute-start(bf16[16,2048]{1,0:T(8,128)(2,1)S(1)} %collective-permute-done.35), channel_id=1, source_target_pairs={{0,15},{1,0},{2,1},{3,2},{4,3},{5,4},{6,5},{7,6},{8,7},{9,8},{10,9... | collective-permute-start | bytes 196616 | tf_op jit(solution)/shard_map/ppermute | solution.py:26
  126.5 18.1 %collective-permute-start.52 = (bf16[16,2048]{1,0:T(8,128)(2,1)S(1)}, bf16[16,2048]{1,0:T(8,128)(2,1)S(1)}, u32[]{:S(2)}, u32[]{:S(2)}) collective-permute-start(bf16[16,2048]{1,0:T(8,128)(2,1)S(1)} %collective-permute-done.50), channel_id=1, source_target_pairs={{0,15},{1,0},{2,1},{3,2},{4,3},{5,4},{6,5},{7,6},{8,7},{9,8},{10,9... | collective-permute-start | bytes 196616 | tf_op jit(solution)/shard_map/ppermute | solution.py:26
  132.6 18.6 %collective-permute-start.7 = (bf16[16,2048]{1,0:T(8,128)(2,1)S(1)}, bf16[16,2048]{1,0:T(8,128)(2,1)S(1)}, u32[]{:S(2)}, u32[]{:S(2)}) collective-permute-start(bf16[16,2048]{1,0:T(8,128)(2,1)S(1)} %collective-permute-done.5), channel_id=1, source_target_pairs={{0,15},{1,0},{2,1},{3,2},{4,3},{5,4},{6,5},{7,6},{8,7},{9,8},{10,9... | collective-permute-start | bytes 196616 | tf_op jit(solution)/shard_map/ppermute | solution.py:26
  137.9 13.9 %collective-permute-start.23 = (bf16[16,2048]{1,0:T(8,128)(2,1)S(1)}, bf16[16,2048]{1,0:T(8,128)(2,1)S(1)}, u32[]{:S(2)}, u32[]{:S(2)}) collective-permute-start(bf16[16,2048]{1,0:T(8,128)(2,1)S(1)} %collective-permute-done.21), channel_id=1, source_target_pairs={{0,1},{1,2},{2,3},{3,4},{4,5},{5,6},{6,7},{7,8},{8,9},{9,10},{10,1... | collective-permute-start | bytes 196616 | tf_op jit(solution)/shard_map/ppermute | solution.py:23
  138.6 19.3 %collective-permute-start.24 = (bf16[16,2048]{1,0:T(8,128)(2,1)S(1)}, bf16[16,2048]{1,0:T(8,128)(2,1)S(1)}, u32[]{:S(2)}, u32[]{:S(2)}) collective-permute-start(bf16[16,2048]{1,0:T(8,128)(2,1)S(1)} %collective-permute-done.22), channel_id=1, source_target_pairs={{0,15},{1,0},{2,1},{3,2},{4,3},{5,4},{6,5},{7,6},{8,7},{9,8},{10,9... | collective-permute-start | bytes 196616 | tf_op jit(solution)/shard_map/ppermute | solution.py:26
  145.2 18.0 %collective-permute-start.39 = (bf16[16,2048]{1,0:T(8,128)(2,1)S(1)}, bf16[16,2048]{1,0:T(8,128)(2,1)S(1)}, u32[]{:S(2)}, u32[]{:S(2)}) collective-permute-start(bf16[16,2048]{1,0:T(8,128)(2,1)S(1)} %collective-permute-done.37), channel_id=1, source_target_pairs={{0,15},{1,0},{2,1},{3,2},{4,3},{5,4},{6,5},{7,6},{8,7},{9,8},{10,9... | collective-permute-start | bytes 196616 | tf_op jit(solution)/shard_map/ppermute | solution.py:26
  151.8 18.1 %collective-permute-start.54 = (bf16[16,2048]{1,0:T(8,128)(2,1)S(1)}, bf16[16,2048]{1,0:T(8,128)(2,1)S(1)}, u32[]{:S(2)}, u32[]{:S(2)}) collective-permute-start(bf16[16,2048]{1,0:T(8,128)(2,1)S(1)} %collective-permute-done.52), channel_id=1, source_target_pairs={{0,15},{1,0},{2,1},{3,2},{4,3},{5,4},{6,5},{7,6},{8,7},{9,8},{10,9... | collective-permute-start | bytes 196616 | tf_op jit(solution)/shard_map/ppermute | solution.py:26
  157.9 18.6 %collective-permute-start.9 = (bf16[16,2048]{1,0:T(8,128)(2,1)S(1)}, bf16[16,2048]{1,0:T(8,128)(2,1)S(1)}, u32[]{:S(2)}, u32[]{:S(2)}) collective-permute-start(bf16[16,2048]{1,0:T(8,128)(2,1)S(1)} %collective-permute-done.7), channel_id=1, source_target_pairs={{0,15},{1,0},{2,1},{3,2},{4,3},{5,4},{6,5},{7,6},{8,7},{9,8},{10,9... | collective-permute-start | bytes 196616 | tf_op jit(solution)/shard_map/ppermute | solution.py:26
  163.2 13.9 %collective-permute-start.25 = (bf16[16,2048]{1,0:T(8,128)(2,1)S(1)}, bf16[16,2048]{1,0:T(8,128)(2,1)S(1)}, u32[]{:S(2)}, u32[]{:S(2)}) collective-permute-start(bf16[16,2048]{1,0:T(8,128)(2,1)S(1)} %collective-permute-done.23), channel_id=1, source_target_pairs={{0,1},{1,2},{2,3},{3,4},{4,5},{5,6},{6,7},{7,8},{8,9},{9,10},{10,1... | collective-permute-start | bytes 196616 | tf_op jit(solution)/shard_map/ppermute | solution.py:23
  164.0 19.5 %collective-permute-start.26 = (bf16[16,2048]{1,0:T(8,128)(2,1)S(1)}, bf16[16,2048]{1,0:T(8,128)(2,1)S(1)}, u32[]{:S(2)}, u32[]{:S(2)}) collective-permute-start(bf16[16,2048]{1,0:T(8,128)(2,1)S(1)} %collective-permute-done.24), channel_id=1, source_target_pairs={{0,15},{1,0},{2,1},{3,2},{4,3},{5,4},{6,5},{7,6},{8,7},{9,8},{10,9... | collective-permute-start | bytes 196616 | tf_op jit(solution)/shard_map/ppermute | solution.py:26
  170.5 18.2 %collective-permute-start.41 = (bf16[16,2048]{1,0:T(8,128)(2,1)S(1)}, bf16[16,2048]{1,0:T(8,128)(2,1)S(1)}, u32[]{:S(2)}, u32[]{:S(2)}) collective-permute-start(bf16[16,2048]{1,0:T(8,128)(2,1)S(1)} %collective-permute-done.39), channel_id=1, source_target_pairs={{0,15},{1,0},{2,1},{3,2},{4,3},{5,4},{6,5},{7,6},{8,7},{9,8},{10,9... | collective-permute-start | bytes 196616 | tf_op jit(solution)/shard_map/ppermute | solution.py:26
  177.1 18.3 %collective-permute-start.56 = (bf16[16,2048]{1,0:T(8,128)(2,1)S(1)}, bf16[16,2048]{1,0:T(8,128)(2,1)S(1)}, u32[]{:S(2)}, u32[]{:S(2)}) collective-permute-start(bf16[16,2048]{1,0:T(8,128)(2,1)S(1)} %collective-permute-done.54), channel_id=1, source_target_pairs={{0,15},{1,0},{2,1},{3,2},{4,3},{5,4},{6,5},{7,6},{8,7},{9,8},{10,9... | collective-permute-start | bytes 196616 | tf_op jit(solution)/shard_map/ppermute | solution.py:26
  183.4 18.6 %collective-permute-start.11 = (bf16[16,2048]{1,0:T(8,128)(2,1)S(1)}, bf16[16,2048]{1,0:T(8,128)(2,1)S(1)}, u32[]{:S(2)}, u32[]{:S(2)}) collective-permute-start(bf16[16,2048]{1,0:T(8,128)(2,1)S(1)} %collective-permute-done.9), channel_id=1, source_target_pairs={{0,15},{1,0},{2,1},{3,2},{4,3},{5,4},{6,5},{7,6},{8,7},{9,8},{10,9... | collective-permute-start | bytes 196616 | tf_op jit(solution)/shard_map/ppermute | solution.py:26
  188.8 13.9 %collective-permute-start.27 = (bf16[16,2048]{1,0:T(8,128)(2,1)S(1)}, bf16[16,2048]{1,0:T(8,128)(2,1)S(1)}, u32[]{:S(2)}, u32[]{:S(2)}) collective-permute-start(bf16[16,2048]{1,0:T(8,128)(2,1)S(1)} %collective-permute-done.25), channel_id=1, source_target_pairs={{0,1},{1,2},{2,3},{3,4},{4,5},{5,6},{6,7},{7,8},{8,9},{9,10},{10,1... | collective-permute-start | bytes 196616 | tf_op jit(solution)/shard_map/ppermute | solution.py:23
  189.5 19.3 %collective-permute-start.28 = (bf16[16,2048]{1,0:T(8,128)(2,1)S(1)}, bf16[16,2048]{1,0:T(8,128)(2,1)S(1)}, u32[]{:S(2)}, u32[]{:S(2)}) collective-permute-start(bf16[16,2048]{1,0:T(8,128)(2,1)S(1)} %collective-permute-done.26), channel_id=1, source_target_pairs={{0,15},{1,0},{2,1},{3,2},{4,3},{5,4},{6,5},{7,6},{8,7},{9,8},{10,9... | collective-permute-start | bytes 196616 | tf_op jit(solution)/shard_map/ppermute | solution.py:26
  196.1 18.0 %collective-permute-start.43 = (bf16[16,2048]{1,0:T(8,128)(2,1)S(1)}, bf16[16,2048]{1,0:T(8,128)(2,1)S(1)}, u32[]{:S(2)}, u32[]{:S(2)}) collective-permute-start(bf16[16,2048]{1,0:T(8,128)(2,1)S(1)} %collective-permute-done.41), channel_id=1, source_target_pairs={{0,15},{1,0},{2,1},{3,2},{4,3},{5,4},{6,5},{7,6},{8,7},{9,8},{10,9... | collective-permute-start | bytes 196616 | tf_op jit(solution)/shard_map/ppermute | solution.py:26
  202.7 13.7 %collective-permute-start.58 = (bf16[16,2048]{1,0:T(8,128)(2,1)S(1)}, bf16[16,2048]{1,0:T(8,128)(2,1)S(1)}, u32[]{:S(2)}, u32[]{:S(2)}) collective-permute-start(bf16[16,2048]{1,0:T(8,128)(2,1)S(1)} %collective-permute-done.56), channel_id=1, source_target_pairs={{0,15},{1,0},{2,1},{3,2},{4,3},{5,4},{6,5},{7,6},{8,7},{9,8},{10,9... | collective-permute-start | bytes 196616 | tf_op jit(solution)/shard_map/ppermute | solution.py:26
  330.9 16.7 %all-to-all-start = ((bf16[60,16,512]{2,0,1:T(8,128)(2,1)}), bf16[60,16,512]{2,0,1:T(8,128)(2,1)S(1)}, u32[]{:S(2)}, u32[]{:S(2)}) async-start(bf16[60,16,512]{2,0,1:T(8,128)(2,1)} %fusion.20), calls=%async_computation | async-start | bytes 2097152 | tf_op jit(solution)/shard_map/all_to_all | solution.py:148
  334.7 101.2 %all-reduce.11.cloned.1.call-start = ((), (), s32[]{:S(2)}) async-start(), calls=%async_computation.8 | async-start | bytes 655360 | tf_op jit(solution)/shard_map/psum | solution.py:123
  338.4 111.9 %all-gather.21.cloned.1.call-start = ((), (), s32[]{:S(2)}) async-start(), calls=%async_computation.4 | async-start | bytes 3145728 | tf_op jit(solution)/shard_map/all_gather | solution.py:149
  352.3 16.6 %all-to-all-start.1 = ((bf16[60,16,512]{2,0,1:T(8,128)(2,1)}), bf16[60,16,512]{2,0,1:T(8,128)(2,1)S(1)}, u32[]{:S(2)}, u32[]{:S(2)}) async-start(bf16[60,16,512]{2,0,1:T(8,128)(2,1)} %fusion.21), calls=%async_computation.1 | async-start | bytes 2097152 | tf_op jit(solution)/shard_map/all_to_all | solution.py:148
  356.0 169.5 %all-gather.23.cloned.1.call-start = ((), (), s32[]{:S(2)}) async-start(), calls=%async_computation.5 | async-start | bytes 3145728 | tf_op jit(solution)/shard_map/all_gather | solution.py:149
  373.7 16.8 %all-to-all-start.2 = ((bf16[60,16,512]{2,0,1:T(8,128)(2,1)}), bf16[60,16,512]{2,0,1:T(8,128)(2,1)S(1)}, u32[]{:S(2)}, u32[]{:S(2)}) async-start(bf16[60,16,512]{2,0,1:T(8,128)(2,1)} %fusion.22), calls=%async_computation.2 | async-start | bytes 2097152 | tf_op jit(solution)/shard_map/all_to_all | solution.py:148
  377.4 222.7 %all-gather.25.cloned.1.call-start = ((), (), s32[]{:S(2)}) async-start(), calls=%async_computation.6 | async-start | bytes 3145728 | tf_op jit(solution)/shard_map/all_gather | solution.py:149
  395.2 51.9 %all-to-all-start.3 = ((bf16[60,16,512]{2,0,1:T(8,128)(2,1)}), bf16[60,16,512]{2,0,1:T(8,128)(2,1)S(1)}, u32[]{:S(2)}, u32[]{:S(2)}) async-start(bf16[60,16,512]{2,0,1:T(8,128)(2,1)} %fusion.23), calls=%async_computation.3 | async-start | bytes 2097152 | tf_op jit(solution)/shard_map/all_to_all | solution.py:148
  398.8 276.1 %all-gather.27.cloned.1.call-start = ((), (), s32[]{:S(2)}) async-start(), calls=%async_computation.7 | async-start | bytes 3145728 | tf_op jit(solution)/shard_map/all_gather | solution.py:149
  (49 other events, 991.7 us)
Sparse Core Ops, SparseCore 0:
  229.9 56.0 all-reduce.12
  339.1 96.8 all-reduce.10
  437.6 12.7 all-gather.20
  451.8 14.6 all-gather.22
  468.0 14.6 all-gather.24
  484.1 14.6 all-gather.26
